TPU v7x, 128 devices: a whole 4x4x4 slice. The times are simulated.
128 devices in a mesh: src: 32 (over y, x_hi, z), sta: 4 (over x_lo, core).
Axes of the slice: x: 4 (x_hi: 2, x_lo: 2; x = x_hi * 2 + x_lo), y: 4, z: 4, core: 2. Of those that a mesh axis runs over, the one named last changes fastest.
Arguments:
- trace: float32 [256, 8256], P('sta', 'src'), may hold values from -6 to 6
- quadrature: float32 [256, 8256], P('sta', 'src'), may hold values from -6 to 6
- gains: float32 [256], P('sta'), may hold values from 0.3 to 3
- lags: int32 [4096, 256], P('src', 'sta'), may hold values from 0 to 63
Outputs:
- beam_power: float32 [2, 4096], P(None, 'src')
All inputs are finite; a program needn't handle non-finite values.
Results may differ from a plain program's by a relative error of at most 0.0003.
Values may be sent and summed in bfloat16 or wider, within the bound.
No kernel may reach another device: no remote copies, remote signals or barrier semaphores. Data moves between devices by JAX's collectives and lax.ppermute only.
A program may use at most 256 MiB of HBM per device.

v0:
```python
import jax
import jax.numpy as jnp
from jax import lax
from jax.sharding import PartitionSpec as P

W = 4096
LAGS = 64
STEPS = 2


def on_device(trace, quadrature, gains, lags):
    energy = trace * trace + quadrature * quadrature
    row_totals = lax.psum(jnp.sum(energy, axis=1), "src")
    baseline = row_totals / (energy.shape[1] * lax.axis_size("src"))
    weighted = (gains[:, None] * (energy - baseline[:, None])).astype(jnp.bfloat16)
    envelope = lax.all_gather(weighted, "src", axis=1, tiled=True)
    cell_count, station_count = lags.shape
    offsets = jnp.arange(LAGS, dtype=jnp.int32)
    selector = (lags[:, None, :] == offsets[None, :, None]).astype(jnp.bfloat16)
    selector = selector.reshape(cell_count, LAGS * station_count)
    power_rows = []
    for step_index in range(STEPS):
        start = step_index * W
        stacked = jnp.concatenate(
            [envelope[:, start + lag_index : start + lag_index + W] for lag_index in range(LAGS)],
            axis=0,
        )
        partial_beam = jnp.dot(selector, stacked, preferred_element_type=jnp.float32)
        beam = lax.psum(partial_beam, "sta")
        power_rows.append(jnp.sum(beam * beam, axis=1))
    power = jnp.stack(power_rows)
    peak_power = lax.pmax(jnp.max(power, axis=1), "src")
    return power / peak_power[:, None]


def solution(mesh):
    return jax.shard_map(
        on_device,
        mesh=mesh,
        in_specs=(P("sta", "src"), P("sta", "src"), P("sta"), P("src", "sta")),
        out_specs=P(None, "src"),
        check_vma=False,
    )
```

profile of v0, /device:TPU:0, one launch (start us, length us, event | category | flops | bytes accessed | tf_op | source)
XLA Modules:
  0.0 483.9 jit_solution(4156925438073581276)
XLA Ops:
  7.6 97.9 %psum.21 = f32[64]{0:T(128)S(1)} all-reduce(f32[64]{0:T(128)S(1)} %fusion.1), channel_id=1, replica_groups=mesh['src'=32,'sta'=4] {'src'}, use_global_device_ids=true, to_apply=%region_1.0 | all-reduce | flops 64 | bytes 512 | tf_op jit(solution)/shard_map/psum | solution.py:13
  105.5 1.7 fusion
  107.3 1.5 bitcast_compare_fusion
  108.8 61.0 %all-gather.3.cloned.1.call-done = bf16[32,258,64]{1,2,0:T(8,128)(2,1)} async-done(((bf16[1,258,64]{1,2,0:T(8,128)(2,1)}), bf16[32,258,64]{1,2,0:T(8,128)(2,1)}) %all-gather.3.cloned.1.call-update) | async-done | bytes 1056784 | tf_op jit(solution)/shard_map/all_gather | solution.py:16
  169.9 2.3 copy.7
  172.2 1.9 reshape.8
  176.1 1.2 slice_dynamic-update-slice_fusion.125
  184.2 1.2 slice_dynamic-update-slice_fusion.118
  190.1 1.2 slice_dynamic-update-slice_fusion.113
  191.3 1.2 slice_dynamic-update-slice_fusion.112
  192.5 1.2 slice_dynamic-update-slice_fusion.111
  194.9 1.2 slice_dynamic-update-slice_fusion.109
  199.5 1.2 slice_dynamic-update-slice_fusion.105
  200.7 1.2 slice_dynamic-update-slice_fusion.104
  204.2 1.2 slice_dynamic-update-slice_fusion.101
  210.1 1.2 slice_dynamic-update-slice_fusion.96
  212.4 1.4 slice_dynamic-update-slice_fusion.94
  221.9 1.2 slice_dynamic-update-slice_fusion.86
  223.1 1.2 slice_dynamic-update-slice_fusion.85
  227.7 1.2 slice_dynamic-update-slice_fusion.81
  228.9 1.2 slice_dynamic-update-slice_fusion.80
  230.1 1.2 slice_dynamic-update-slice_fusion.79
  232.5 1.2 slice_dynamic-update-slice_fusion.77
  237.1 1.2 slice_dynamic-update-slice_fusion.73
  238.3 1.2 slice_dynamic-update-slice_fusion.72
  246.5 1.2 slice_dynamic-update-slice_fusion.65
  248.8 11.1 %copy-done = bf16[4096,4096]{1,0:T(8,128)(2,1)} copy-done((bf16[4096,4096]{1,0:T(8,128)(2,1)}, bf16[4096,4096]{1,0:T(8,128)(2,1)S(1)}, u32[]{:S(2)}) %copy-start) | copy-done | bytes 33554456
  259.9 14.4 %fusion.3 = f32[128,4096]{1,0:T(8,128)} fusion(pred[128,4096]{0,1:T(32,128)(4,1)S(1)} %bitcast_compare_fusion, bf16[4096,4096]{1,0:T(8,128)(2,1)} %copy-done), kind=kOutput, calls=%fused_computation.139 | convolution fusion | flops 4294967296 | bytes 36175872 | tf_op jit(solution)/shard_map/dot_general | solution.py:28
  274.3 14.3 %fusion.4 = f32[128,4096]{1,0:T(8,128)} fusion(pred[128,4096]{0,1:T(32,128)(4,1)S(1)} %bitcast_compare_fusion, bf16[4096,4096]{1,0:T(8,128)(2,1)} %get-tuple-element.8), kind=kOutput, calls=%fused_computation.140 | convolution fusion | flops 4294967296 | bytes 36175872 | tf_op jit(solution)/shard_map/dot_general | solution.py:28
  288.6 89.0 %all-reduce.3.cloned.1.call-done = (f32[128,4096]{1,0:T(8,128)}, f32[128,4096]{1,0:T(8,128)}) async-done(((f32[128,4096]{1,0:T(8,128)}, f32[128,4096]{1,0:T(8,128)}), (f32[128,4096]{1,0:T(8,128)}, f32[128,4096]{1,0:T(8,128)})) %all-reduce.3.cloned.1.call-update) | async-done | bytes 4194320 | tf_op jit(solution)/shard_map/psum | solution.py:29
  377.6 2.6 multiply_reduce_fusion
  380.3 96.1 %pmax.7 = f32[2]{0:T(128)S(1)} all-reduce(f32[2]{0:T(128)S(1)} %fusion.2), channel_id=1, replica_groups=mesh['src'=32,'sta'=4] {'src'}, use_global_device_ids=true, to_apply=%region_7.0 | all-reduce | flops 2 | bytes 16 | tf_op jit(solution)/shard_map/pmax | solution.py:32
  (55 shorter events, 52.7 us)
Async XLA Ops:
  6.5 163.3 %all-gather.3.cloned.1.call-start = ((), (), s32[]{:S(2)}) async-start(), calls=%async_computation | async-start | bytes 1622016 | tf_op jit(solution)/shard_map/all_gather | solution.py:16
  107.2 270.4 %all-reduce.3.cloned.1.call-start = ((), (), s32[]{:S(2)}) async-start(), calls=%async_computation.1 | async-start | bytes 8388608 | tf_op jit(solution)/shard_map/psum | solution.py:29
  248.8 11.1 %copy-start = (bf16[4096,4096]{1,0:T(8,128)(2,1)}, bf16[4096,4096]{1,0:T(8,128)(2,1)S(1)}, u32[]{:S(2)}) copy-start(bf16[4096,4096]{1,0:T(8,128)(2,1)S(1)} %get-tuple-element.7) | copy-start | bytes 100663296
Sparse Core Ops, SparseCore 0:
  107.3 62.4 all-gather.2
  288.8 88.8 all-reduce.2
where the time goes:
time: 484 us
  blocking collectives  194 us (40%)
  waiting for transfers between devices  150 us (31%)
  local copies, waits for them, and re-layouts  90.1 us (19%)
  matrix products  28.7 us (6%)
  between operations  13.5 us (3%)
  other arithmetic  7.54 us (2%)
    psum x1, blocking collectives, on_device(): row_totals = lax.psum(jnp.sum(energy, axis=1), 'src')  97.9 us
    pmax x1, blocking collectives, on_device(): peak_power = lax.pmax(jnp.max(power, axis=1), 'src')  96.1 us
    psum x1, waiting for transfers between devices, on_device(): beam = lax.psum(partial_beam, 'sta')  89 us
    unnamed x66, local copies, waits for them, and re-layouts  86.5 us
    all_gather x1, waiting for transfers between devices, on_device(): envelope = lax.all_gather(weighted, 'src', axis=1, tiled=True)  61 us
    dot_general x2, matrix products, on_device(): jnp.dot(selector, stacked, preferred_element_type=jnp.float32)  28.7 us
  transfers between devices with their start and end apart: 2, of which 2 were waited for; matrix products, arithmetic and copies ran while one was open for 0% of the time, Pallas kernels for 0%

commit v1 on v0

--- a/solution.py
+++ b/solution.py
@@ -2,6 +2,7 @@
 import jax.numpy as jnp
 from jax import lax
 from jax.sharding import PartitionSpec as P
+from jax.lax import all_to_all, axis_size
 
 W = 4096
 LAGS = 64
@@ -13,7 +14,10 @@
     row_totals = lax.psum(jnp.sum(energy, axis=1), "src")
     baseline = row_totals / (energy.shape[1] * lax.axis_size("src"))
     weighted = (gains[:, None] * (energy - baseline[:, None])).astype(jnp.bfloat16)
-    envelope = lax.all_gather(weighted, "src", axis=1, tiled=True)
+    envelope = jnp.concatenate(
+        all_to_all(jnp.stack([weighted for _ in range(axis_size("src"))], axis=0), "src", 0, 0),
+        axis=1,
+    )
     cell_count, station_count = lags.shape
     offsets = jnp.arange(LAGS, dtype=jnp.int32)
     selector = (lags[:, None, :] == offsets[None, :, None]).astype(jnp.bfloat16)

time: 484 us -> 443 us (0.915)
  waiting for transfers between devices: 150 us -> 103 us
    all_gather x1 -> x0, waiting for transfers between devices: 61 us -> none  [on_device(): envelope = lax.all_gather(weighted, 'src', axis=1, tiled=True)]
    all_to_all x0 -> x1, waiting for transfers between devices: none -> 14.8 us  [on_device(): all_to_all(jnp.stack([weighted for _ in range(axis_size('src'))], axis=0)...]
    reshape x0 -> x2, local copies, waits for them, and re-layouts: none -> 5.37 us  [on_device(): jnp.concatenate(all_to_all(jnp.stack([weighted for _ in range(axis_size('...]
    unnamed x66 -> x65, local copies, waits for them, and re-layouts: 86.5 us -> 84.9 us
where the time goes in v1:
time: 443 us
  blocking collectives  194 us (44%)
  waiting for transfers between devices  103 us (23%)
  local copies, waits for them, and re-layouts  92.9 us (21%)
  matrix products  28.7 us (6%)
  between operations  13.5 us (3%)
  other arithmetic  6.92 us (2%)
    psum x1, blocking collectives, on_device(): row_totals = lax.psum(jnp.sum(energy, axis=1), 'src')  97.9 us
    pmax x1, blocking collectives, on_device(): peak_power = lax.pmax(jnp.max(power, axis=1), 'src')  96.1 us
    psum x1, waiting for transfers between devices, on_device(): beam = lax.psum(partial_beam, 'sta')  88.1 us
    unnamed x65, local copies, waits for them, and re-layouts  84.9 us
    dot_general x2, matrix products, on_device(): jnp.dot(selector, stacked, preferred_element_type=jnp.float32)  28.7 us
    all_to_all x1, waiting for transfers between devices, on_device(): all_to_all(jnp.stack([weighted for _ in range(axis_size('src'))], axis=0)...  14.8 us
  transfers between devices with their start and end apart: 2, of which 2 were waited for; matrix products, arithmetic and copies ran while one was open for 0% of the time, Pallas kernels for 0%

profile of v1, /device:TPU:0, one launch (start us, length us, event | category | flops | bytes accessed | tf_op | source)
XLA Modules:
  0.0 443.0 jit_solution(3545723839941779984)
XLA Ops:
  7.6 97.9 %psum.21 = f32[64]{0:T(128)S(1)} all-reduce(f32[64]{0:T(128)S(1)} %fusion), channel_id=1, replica_groups=mesh['src'=32,'sta'=4] {'src'}, use_global_device_ids=true, to_apply=%region_1.0 | all-reduce | flops 64 | bytes 512 | tf_op jit(solution)/shard_map/psum | solution.py:14
  106.6 1.4 stack.8
  108.0 4.0 all-to-all-start
  112.1 1.5 bitcast_compare_fusion
  113.6 14.8 %all-to-all-done = bf16[32,64,258]{2,1,0:T(8,128)(2,1)S(1)} async-done(((bf16[32,64,258]{2,1,0:T(8,128)(2,1)}), bf16[32,64,258]{2,1,0:T(8,128)(2,1)S(1)}, u32[]{:S(2)}, u32[]{:S(2)}) %all-to-all-start) | async-done | bytes 1056800 | tf_op jit(solution)/shard_map/all_to_all | solution.py:18
  128.4 2.1 copy.6
  130.5 3.3 reshape.16
  134.7 1.2 slice_dynamic-update-slice_fusion.126
  135.9 1.2 slice_dynamic-update-slice_fusion.125
  149.9 1.2 slice_dynamic-update-slice_fusion.113
  151.1 1.2 slice_dynamic-update-slice_fusion.112
  152.3 1.2 slice_dynamic-update-slice_fusion.111
  154.6 1.2 slice_dynamic-update-slice_fusion.109
  159.3 1.2 slice_dynamic-update-slice_fusion.105
  160.5 1.2 slice_dynamic-update-slice_fusion.104
  161.7 1.2 slice_dynamic-update-slice_fusion.103
  172.2 1.4 slice_dynamic-update-slice_fusion.94
  181.8 1.2 slice_dynamic-update-slice_fusion.86
  187.6 1.2 slice_dynamic-update-slice_fusion.81
  188.8 1.2 slice_dynamic-update-slice_fusion.80
  190.0 1.2 slice_dynamic-update-slice_fusion.79
  192.4 1.2 slice_dynamic-update-slice_fusion.77
  197.0 1.2 slice_dynamic-update-slice_fusion.73
  198.2 1.2 slice_dynamic-update-slice_fusion.72
  199.4 1.2 slice_dynamic-update-slice_fusion.71
  206.5 1.2 slice_dynamic-update-slice_fusion.65
  208.8 11.1 %copy-done = bf16[4096,4096]{1,0:T(8,128)(2,1)} copy-done((bf16[4096,4096]{1,0:T(8,128)(2,1)}, bf16[4096,4096]{1,0:T(8,128)(2,1)S(1)}, u32[]{:S(2)}) %copy-start) | copy-done | bytes 33554456
  219.8 14.4 %fusion.2 = f32[128,4096]{1,0:T(8,128)} fusion(pred[128,4096]{0,1:T(32,128)(4,1)S(1)} %bitcast_compare_fusion, bf16[4096,4096]{1,0:T(8,128)(2,1)} %copy-done), kind=kOutput, calls=%fused_computation.138 | convolution fusion | flops 4294967296 | bytes 36175872 | tf_op jit(solution)/shard_map/dot_general | solution.py:32
  234.2 14.3 %fusion.3 = f32[128,4096]{1,0:T(8,128)} fusion(pred[128,4096]{0,1:T(32,128)(4,1)S(1)} %bitcast_compare_fusion, bf16[4096,4096]{1,0:T(8,128)(2,1)} %get-tuple-element.8), kind=kOutput, calls=%fused_computation.139 | convolution fusion | flops 4294967296 | bytes 36175872 | tf_op jit(solution)/shard_map/dot_general | solution.py:32
  248.6 88.1 %all-reduce.3.cloned.1.call-done = (f32[128,4096]{1,0:T(8,128)}, f32[128,4096]{1,0:T(8,128)}) async-done(((f32[128,4096]{1,0:T(8,128)}, f32[128,4096]{1,0:T(8,128)}), (f32[128,4096]{1,0:T(8,128)}, f32[128,4096]{1,0:T(8,128)})) %all-reduce.3.cloned.1.call-update) | async-done | bytes 4194320 | tf_op jit(solution)/shard_map/psum | solution.py:33
  336.7 2.6 multiply_reduce_fusion
  339.4 96.1 %pmax.7 = f32[2]{0:T(128)S(1)} all-reduce(f32[2]{0:T(128)S(1)} %fusion.1), channel_id=1, replica_groups=mesh['src'=32,'sta'=4] {'src'}, use_global_device_ids=true, to_apply=%region_7.0 | all-reduce | flops 2 | bytes 16 | tf_op jit(solution)/shard_map/pmax | solution.py:36
  (55 shorter events, 55.1 us)
Async XLA Ops:
  108.0 20.4 %all-to-all-start = ((bf16[32,64,258]{2,1,0:T(8,128)(2,1)}), bf16[32,64,258]{2,1,0:T(8,128)(2,1)S(1)}, u32[]{:S(2)}, u32[]{:S(2)}) async-start(bf16[32,64,258]{2,1,0:T(8,128)(2,1)} %stack.8), calls=%async_computation | async-start | bytes 3145728 | tf_op jit(solution)/shard_map/all_to_all | solution.py:18
  112.0 224.7 %all-reduce.3.cloned.1.call-start = ((), (), s32[]{:S(2)}) async-start(), calls=%async_computation.1 | async-start | bytes 8388608 | tf_op jit(solution)/shard_map/psum | solution.py:33
  208.8 11.1 %copy-start = (bf16[4096,4096]{1,0:T(8,128)(2,1)}, bf16[4096,4096]{1,0:T(8,128)(2,1)S(1)}, u32[]{:S(2)}) copy-start(bf16[4096,4096]{1,0:T(8,128)(2,1)S(1)} %get-tuple-element.7) | copy-start | bytes 100663296
Sparse Core Ops, SparseCore 0:
  248.7 87.9 all-reduce.2
